TPU v7x, 512 devices: a whole 4x4x16 slice. The times are simulated.
512 devices in a mesh: ctx: 64 (over z, x), head: 8 (over y, core).
Axes of the slice: x: 4, y: 4, z: 16, core: 2. Of those that a mesh axis runs over, the one named last changes fastest.
Arguments:
- document_query: bfloat16 [16384, 8192], P('ctx', 'head'), may hold values from -6 to 6
- document_keys: bfloat16 [16384, 1024], P('ctx', 'head'), may hold values from -4 to 4
- document_values: bfloat16 [16384, 1024], P('ctx', 'head'), may hold values from -6 to 6
- question_query: bfloat16 [128, 8192], P(None, 'head'), may hold values from -10 to 10
- prompt_keys: bfloat16 [128, 1024], P(None, 'head'), may hold values from -6 to 6
- prompt_values: bfloat16 [128, 1024], P(None, 'head'), may hold values from -6 to 6
- out_weight: bfloat16 [8192, 8192], P('head', 'ctx'), may hold values from -0.0625 to 0.0625
Outputs:
- doc_attention: bfloat16 [16384, 8192], P('ctx', 'head')
- question_out: bfloat16 [128, 8192], P('head', 'ctx')
All inputs are finite; a program needn't handle non-finite values.
Results may differ from a plain program's by a relative error of at most 0.014.
Values may be sent and summed in bfloat16 or wider, within the bound.
A program may use at most 64 MiB of HBM per device.

v0:
```python
import jax
import jax.numpy as jnp
from jax import lax
from jax.sharding import PartitionSpec as P

HEAD_SIZE = 128


def from_root(block, axis, source):
    block = jnp.where(lax.axis_index(axis) == source, block, jnp.zeros_like(block))
    return lax.psum(block, axis)


def pair_scores(query_rows, key_rows, factor):
    return (
        lax.dot_general(
            query_rows, key_rows, (((1,), (1,)), ((), ())), preferred_element_type=jnp.float32
        )
        * factor
    )


def rescale(values, weights):
    row_count, head_count = weights.shape
    return (values.reshape(row_count, head_count, -1) * weights[:, :, None]).reshape(row_count, -1)


def combine_parts(first_part, second_part):
    max_one, total_one, sums_one = first_part
    max_two, total_two, sums_two = second_part
    joined = jnp.maximum(max_one, max_two)
    weight_one = jnp.exp(max_one - joined)
    weight_two = jnp.exp(max_two - joined)
    return (
        joined,
        total_one * weight_one + total_two * weight_two,
        rescale(sums_one, weight_one) + rescale(sums_two, weight_two),
    )


def normalized(parts):
    row_top, totals, partial_sums = parts
    return rescale(partial_sums, 1.0 / totals).astype(jnp.bfloat16)


def self_mask(row_span, key_total):
    row_ids = jnp.arange(row_span, dtype=jnp.int32)
    column_ids = jnp.arange(key_total, dtype=jnp.int32)
    return row_ids[:, None] >= column_ids[None, :]


def attend_parts(query_rows, key_block, value_block, visible, factor):
    row_count = query_rows.shape[0]
    head_count = query_rows.shape[1] // HEAD_SIZE

    def single_head(head_at, carried):
        maxima, totals, partial_sums = carried
        head_queries = lax.dynamic_slice_in_dim(query_rows, head_at * HEAD_SIZE, HEAD_SIZE, 1)
        scores = pair_scores(head_queries, key_block, factor)
        if visible is not None:
            scores = jnp.where(visible, scores, -jnp.inf)
        row_top = scores.max(axis=1, keepdims=True)
        exp_scores = jnp.exp(scores - row_top)
        maxima = lax.dynamic_update_slice_in_dim(maxima, row_top, head_at, 1)
        totals = lax.dynamic_update_slice_in_dim(
            totals, exp_scores.sum(axis=1, keepdims=True), head_at, 1
        )
        weighted = jnp.dot(
            exp_scores.astype(jnp.bfloat16), value_block, preferred_element_type=jnp.float32
        )
        partial_sums = lax.dynamic_update_slice_in_dim(
            partial_sums, weighted, head_at * HEAD_SIZE, 1
        )
        return (maxima, totals, partial_sums)

    start_parts = (
        jnp.zeros((row_count, head_count), jnp.float32),
        jnp.zeros((row_count, head_count), jnp.float32),
        jnp.zeros((row_count, head_count * HEAD_SIZE), jnp.float32),
    )
    return lax.fori_loop(0, head_count, single_head, start_parts)


def local(
    document_query,
    document_keys,
    document_values,
    question_query,
    prompt_keys,
    prompt_values,
    out_weight,
):
    factor = HEAD_SIZE ** (-0.5)
    block_rows = document_query.shape[0]
    head_count = document_query.shape[1] // HEAD_SIZE
    question_rows = question_query.shape[0]
    position = lax.axis_index("ctx")
    leading_keys, leading_values = (
        from_root(document_keys, "ctx", 0),
        from_root(document_values, "ctx", 0),
    )
    block_ids = jnp.arange(block_rows, dtype=jnp.int32)
    causal = block_ids[:, None] >= block_ids[None, :]

    def doc_head(head_at, written):
        query_rows = lax.dynamic_slice_in_dim(document_query, head_at * HEAD_SIZE, HEAD_SIZE, 1)
        anchor_scores = jnp.where(
            position > 0, pair_scores(query_rows, leading_keys, factor), -jnp.inf
        )
        own_scores = jnp.where(causal, pair_scores(query_rows, document_keys, factor), -jnp.inf)
        row_top = jnp.maximum(
            anchor_scores.max(axis=1, keepdims=True), own_scores.max(axis=1, keepdims=True)
        )
        anchor_exp = jnp.exp(anchor_scores - row_top)
        own_exp = jnp.exp(own_scores - row_top)
        denominator = anchor_exp.sum(axis=1, keepdims=True) + own_exp.sum(axis=1, keepdims=True)
        mixture = jnp.dot(
            anchor_exp.astype(jnp.bfloat16), leading_values, preferred_element_type=jnp.float32
        )
        mixture = mixture + jnp.dot(
            own_exp.astype(jnp.bfloat16), document_values, preferred_element_type=jnp.float32
        )
        return lax.dynamic_update_slice_in_dim(
            written, (mixture / denominator).astype(jnp.bfloat16), head_at * HEAD_SIZE, 1
        )

    doc_attention = lax.fori_loop(0, head_count, doc_head, jnp.zeros_like(document_query))
    block_parts = attend_parts(question_query, document_keys, document_values, None, factor)
    block_max, block_total, block_sums = block_parts
    row_top = lax.pmax(block_max, "ctx")
    weights = jnp.exp(block_max - row_top)
    totals, partial_sums = lax.psum((block_total * weights, rescale(block_sums, weights)), "ctx")
    visible = self_mask(question_rows, prompt_keys.shape[0])
    self_parts = attend_parts(question_query, prompt_keys, prompt_values, visible, factor)
    attention = normalized(combine_parts((row_top, totals, partial_sums), self_parts))
    question_out = lax.psum_scatter(
        jnp.dot(attention, out_weight, preferred_element_type=jnp.float32).astype(jnp.bfloat16),
        "head",
        scatter_dimension=0,
        tiled=True,
    )
    return (doc_attention, question_out)


def solution(mesh):
    placed = (
        P("ctx", "head"),
        P("ctx", "head"),
        P("ctx", "head"),
        P(None, "head"),
        P(None, "head"),
        P(None, "head"),
        P("head", "ctx"),
    )
    return jax.shard_map(
        local,
        mesh=mesh,
        in_specs=placed,
        out_specs=(P("ctx", "head"), P("head", "ctx")),
        check_vma=False,
    )
```

profile of v0, /device:TPU:1, one launch (start us, length us, event | category | flops | bytes accessed | tf_op | source)
XLA Modules:
  0.0 738.7 jit_solution(5080807263460077784)
XLA Ops:
  8.1 12.2 %while.51 = (s32[]{:T(128)}, f32[128,8]{0,1:T(8,128)S(1)}, f32[128,8]{0,1:T(8,128)S(1)}, f32[128,1024]{1,0:T(8,128)S(1)}, bf16[128,1024]{1,0:T(8,128)(2,1)}, /*i...) while((s32[]{:T(128)}, f32[128,8]{0,1:T(8,128)S(1)}, ...), condition=%wide.region_11.12_spmd, body=%wide.region_8.11_spmd.sunk | while | flops 16973572 | bytes 626867 | solution.py:81
  8.1 1.0 fusion.80
  9.6 1.0 fusion.80
  11.2 1.0 fusion.80
  12.7 1.0 fusion.80
  14.2 1.0 fusion.80
  15.7 1.0 fusion.80
  17.3 1.0 fusion.80
  18.8 1.0 fusion.80
  20.3 122.6 %pmax.7 = f32[128,8]{0,1:T(8,128)S(1)} all-reduce(f32[128,8]{0,1:T(8,128)S(1)} %get-tuple-element.483), channel_id=1, replica_groups=mesh['ctx'=64,'head'=8] {'ctx'}, use_global_device_ids=true, to_apply=%region_12.13 | all-reduce | flops 1024 | bytes 8192 | tf_op jit(solution)/shard_map/pmax | solution.py:130
  145.8 10.1 %while.53 = (s32[]{:T(128)}, f32[128,8]{0,1:T(8,128)S(1)}, f32[128,8]{0,1:T(8,128)S(1)}, f32[128,1024]{1,0:T(8,128)S(1)}, bf16[128,1024]{1,0:T(8,128)(2,1)}, /*i...) while((s32[]{:T(128)}, f32[128,8]{0,1:T(8,128)S(1)}, ...), condition=%wide.region_17.18_spmd.clone, body=%wide.region_14.17_spmd.clone.sunk | while | flops 8519430 | bytes 364723 | solution.py:81
  155.9 110.9 %psum.31 = f32[128,8]{0,1:T(8,128)S(1)} all-reduce(f32[128,8]{0,1:T(8,128)S(1)} %get-tuple-element.573), channel_id=1, replica_groups=mesh['ctx'=64,'head'=8] {'ctx'}, use_global_device_ids=true, to_apply=%region_18.19 | all-reduce | flops 1024 | bytes 8192 | tf_op jit(solution)/shard_map/psum | solution.py:132
  267.1 156.6 %all-reduce.4.cloned.1.call-done = f32[128,1024]{1,0:T(8,128)} async-done(((f32[128,1024]{1,0:T(8,128)}), f32[128,1024]{1,0:T(8,128)}) %all-reduce.4.cloned.1.call-update) | async-done | bytes 524304 | tf_op jit(solution)/shard_map/psum | solution.py:132
  425.9 261.2 %all-reduce.6.cloned.1.call-done = (bf16[256,128]{1,0:T(8,128)(2,1)}, bf16[256,128]{1,0:T(8,128)(2,1)}) async-done(((bf16[256,128]{1,0:T(8,128)(2,1)}, bf16[256,128]{1,0:T(8,128)(2,1)}), (bf16[256,128]{1,0:T(8,128)(2,1)}, bf16[256,128]{1,0:T(8,128)(2,1)})) %all-reduce.6.cloned.1.call-update) | async-done | bytes 131088 | tf_op jit(solution)/shard_map/psum | solution.py:11
  688.0 22.2 %while.52 = (s32[]{:T(128)}, bf16[256,1024]{1,0:T(8,128)(2,1)S(1)}, pred[]{:T(512)}, bf16[256,1024]{1,0:T(8,128)(2,1)}, bf16[256,128]{1,0:T(8,128)(2,1)S(1)}, /*...) while((s32[]{:T(128)}, bf16[256,1024]{1,0:T(8,128)(2,1)S(1)}, ...), condition=%wide.region_7.8_spmd.clone, body=%wide.region_2.7_spmd.clone.sunk | while | flops 68189696 | bytes 2308783 | solution.py:127
  688.0 1.1 fusion.89
  689.1 1.1 fusion.88
  690.8 1.1 fusion.89
  691.8 1.1 fusion.88
  693.6 1.1 fusion.89
  694.6 1.1 fusion.88
  696.3 1.1 fusion.89
  697.4 1.1 fusion.88
  699.1 1.1 fusion.89
  700.2 1.1 fusion.88
  701.9 1.1 fusion.89
  702.9 1.1 fusion.88
  704.7 1.1 fusion.89
  705.7 1.1 fusion.88
  707.4 1.1 fusion.89
  708.5 1.1 fusion.88
  710.2 22.0 %reduce-scatter.2.cloned.1.call-done = bf16[16,128]{1,0:T(8,128)(2,1)} async-done(((bf16[128,128]{1,0:T(8,128)(2,1)}), bf16[16,128]{1,0:T(8,128)(2,1)}) %reduce-scatter.2.cloned.1.call-update) | async-done | bytes 4112 | tf_op jit(solution)/shard_map/reduce_scatter | solution.py:136
  (156 shorter events, 25.6 us)
Async XLA Ops:
  7.2 417.1 %copy-start = (bf16[1024,128]{1,0:T(8,128)(2,1)S(1)}, bf16[1024,128]{1,0:T(8,128)(2,1)}, u32[]{:S(2)}) copy-start(bf16[1024,128]{1,0:T(8,128)(2,1)} %param.19) | copy-start | bytes 786436
  7.2 416.5 %all-reduce.4.cloned.1.call-start = ((), (), s32[]{:S(2)}) async-start(), calls=%async_computation.1 | async-start | bytes 1048576 | tf_op jit(solution)/shard_map/psum | solution.py:132
  7.2 0.8 copy-start.1
  7.3 0.9 copy-start.2
  144.2 543.0 %all-reduce.6.cloned.1.call-start = ((), (), s32[]{:S(2)}) async-start(), calls=%async_computation.3 | async-start | bytes 262144 | tf_op jit(solution)/shard_map/psum | solution.py:11
  144.9 587.3 %reduce-scatter.2.cloned.1.call-start = ((), (), s32[]{:S(2)}) async-start(), calls=%async_computation.2 | async-start | bytes 36864 | tf_op jit(solution)/shard_map/reduce_scatter | solution.py:136
  145.0 0.8 copy-start.5
  145.0 0.8 copy-start.6
  423.9 1.0 copy-start.8
  687.1 0.8 copy-start.3
  687.1 0.9 copy-start.4
  710.2 22.0 %copy-start.7 = (bf16[256,1024]{1,0:T(8,128)(2,1)}, bf16[256,1024]{1,0:T(8,128)(2,1)S(1)}, u32[]{:S(2)}) copy-start(bf16[256,1024]{1,0:T(8,128)(2,1)S(1)} %get-tuple-element.479) | copy-start | bytes 1572868
Sparse Core Ops, SparseCore 0:
  144.3 279.3 all-reduce.3
  427.2 259.9 all-reduce.5
  690.5 41.6 reduce-scatter.1
where the time goes:
time: 741 us; the launch traced here: 739 us
  waiting for transfers between devices  440 us (59%)
  blocking collectives  234 us (32%)
  matrix products  40.8 us (6%)
  between operations  13.9 us (2%)
    psum x1, waiting for transfers between devices, from_root(): return lax.psum(block, axis)  261 us
    psum x1, waiting for transfers between devices, local(): lax.psum((block_total * weights, rescale(block_sums, weights)), 'ctx')  157 us
    pmax x1, blocking collectives, local(): row_top = lax.pmax(block_max, 'ctx')  123 us
    psum x1, blocking collectives, local(): lax.psum((block_total * weights, rescale(block_sums, weights)), 'ctx')  111 us
    dot_general x32, matrix products, pair_scores(): lax.dot_general(query_rows, key_rows, (((1,), (1,)), ((), ())), preferred...  32.6 us
    reduce_scatter x1, waiting for transfers between devices, local(): lax.psum_scatter(jnp.dot(attention, out_weight, preferred_element_type=jn...  22 us
  transfers between devices with their start and end apart: 3, of which 3 were waited for; matrix products, arithmetic and copies ran while one was open for 5% of the time, Pallas kernels for 0%

commit v1 on v0

v1 whole, which is shorter than its diff:
```python
import functools
import math

import jax
import jax.numpy as jnp
from jax import lax
from jax.experimental import pallas as pl
from jax.experimental.pallas import tpu as pltpu
from jax.sharding import PartitionSpec as P

HEAD_SIZE = 128
LOG2E = math.log2(math.e)
SCALE2 = HEAD_SIZE**-0.5 * LOG2E
NEG_INF = float("-inf")
BF16 = jnp.bfloat16
F32 = jnp.float32
MESH = pl.DeviceIdType.MESH


def dot_nt(a, b):
    return lax.dot_general(a, b, (((1,), (1,)), ((), ())), preferred_element_type=F32)


def dot_nn(a, b):
    return jnp.dot(a, b, preferred_element_type=F32)


def by_distance(n):
    return sorted(range(1, n), key=lambda d: -min(d, n - d))


def kernel(
    nx, nz, nh,
    dq_hbm, k_hbm, v_hbm, qq_hbm, pk_hbm, pv_hbm, w_hbm,
    doc_ref, out_ref,
    dq, kb, vb, qq, pk, pv, wb, wt, vt,
    xs, xr, xst, xrt, zs, zr, zst, zrt, att, hs, hr,
    self_o, self_s, own_o, own_s, anc, vat,
    in_sem, xd_send, xd_recv, xt_send, xt_recv,
    zd_send, zd_recv, zt_send, zt_recv,
    gz_send, gz_recv, gx_send, gx_recv, h_send, h_recv,
    ar_send, az_send, ax_send, a_recv,
):
    ctx = lax.axis_index("ctx")
    head = lax.axis_index("head")
    x = lax.rem(ctx, nx)
    z = ctx // nx
    heads = qq.shape[1] // HEAD_SIZE
    hpx = heads // nx
    rows = xs.shape[2]
    n_q = qq.shape[0]
    block = kb.shape[0]
    pieces_per_head = HEAD_SIZE // rows

    def x_peer(d):
        return lax.rem(x + d, nx)

    def z_peer(d):
        return lax.rem(z + d, nz)

    def at(zi, xi):
        return {"ctx": zi * nx + xi}

    loads = [
        pltpu.make_async_copy(src, dst, in_sem.at[i])
        for i, (src, dst) in enumerate(
            ((k_hbm, kb), (qq_hbm, qq), (v_hbm, vb), (dq_hbm, dq), (pk_hbm, pk), (pv_hbm, pv), (w_hbm, wb))
        )
    ]
    for load in loads:
        load.start()

    barrier = pltpu.get_barrier_semaphore()
    for d in by_distance(nz):
        pl.semaphore_signal(barrier, inc=1, device_id=at(z_peer(d), x), device_id_type=MESH)
    for d in by_distance(nx):
        pl.semaphore_signal(barrier, inc=1, device_id=at(z, x_peer(d)), device_id_type=MESH)
    for d in range(1, nh):
        pl.semaphore_signal(
            barrier, inc=1, device_id={"head": lax.rem(head + d, nh)}, device_id_type=MESH
        )

    loads[0].wait()
    loads[1].wait()
    loads[2].wait()
    vt[...] = vb[...].T

    def question_group(d, data, stats):
        first = x_peer(d) * hpx
        for i in range(hpx):
            lanes = pl.ds(pl.multiple_of((first + i) * HEAD_SIZE, HEAD_SIZE), HEAD_SIZE)
            s = dot_nt(kb[...], qq[:, lanes]) * SCALE2
            top = s.max(axis=0, keepdims=True)
            p = jnp.exp2(s - top)
            total = p.sum(axis=0, keepdims=True)
            sums = dot_nn(vt[...], p.astype(BF16)).astype(BF16)
            for j in range(pieces_per_head):
                data[d, i * pieces_per_head + j] = sums[j * rows : (j + 1) * rows]
            stats[d, i, 0:1] = top
            stats[d, i, 1:2] = total

    for d in by_distance(nx):
        question_group(d, xs, xst)
    question_group(0, xr, xrt)

    key_at = lax.broadcasted_iota(jnp.int32, (block, block), 0)
    row_at = lax.broadcasted_iota(jnp.int32, (block, block), 1)

    def own_head(h, carry):
        lanes = pl.ds(pl.multiple_of(h * HEAD_SIZE, HEAD_SIZE), HEAD_SIZE)
        s = dot_nt(kb[...], dq[:, lanes]) * SCALE2
        s = jnp.where(key_at <= row_at, s, NEG_INF)
        top = s.max(axis=0, keepdims=True)
        p = jnp.exp2(s - top)
        own_s[h, 0:1] = top
        own_s[h, 1:2] = p.sum(axis=0, keepdims=True)
        own_o[h] = dot_nn(vt[...], p.astype(BF16))
        return carry

    def anchored_head(h, carry):
        lanes = pl.ds(pl.multiple_of(h * HEAD_SIZE, HEAD_SIZE), HEAD_SIZE)
        s = dot_nt(anc[0 : nx // 2].reshape(block, HEAD_SIZE), dq[:, lanes]) * SCALE2
        s = jnp.where(ctx > 0, s, NEG_INF)
        own_top = own_s[h, 0:1]
        top = jnp.maximum(s.max(axis=0, keepdims=True), own_top)
        p = jnp.exp2(s - top)
        keep = jnp.exp2(own_top - top)
        total = own_s[h, 1:2] * keep + p.sum(axis=0, keepdims=True)
        o = own_o[h] * keep + dot_nn(vat[...], p.astype(BF16))
        doc_ref[:, lanes] = (o * (1.0 / total)).T.astype(BF16)
        return carry

    loads[3].wait()
    lax.fori_loop(0, 2, own_head, 0)

    pl.semaphore_wait(barrier, (nx - 1) + (nz - 1) + (nh - 1))

    x_copies = []
    for d in by_distance(nx):
        peer = at(z, x_peer(d))
        for src, dst, send, recv in ((xst, xrt, xt_send, xt_recv), (xs, xr, xd_send, xd_recv)):
            copy = pltpu.make_async_remote_copy(
                src_ref=src.at[d], dst_ref=dst.at[d], send_sem=send.at[d], recv_sem=recv.at[d],
                device_id=peer, device_id_type=MESH,
            )
            copy.start()
            x_copies.append(copy)

    a_rows = anc.shape[1]

    def anchor_source(j):
        src = k_hbm if j < nx // 2 else v_hbm
        return src.at[pl.ds((j % (nx // 2)) * a_rows, a_rows)]

    anchor_local = pltpu.make_async_copy(anchor_source(0), anc.at[0], a_recv.at[0])
    root_copies = [
        pltpu.make_async_remote_copy(
            src_ref=anchor_source(j), dst_ref=anc.at[j], send_sem=ar_send.at[j], recv_sem=a_recv.at[j],
            device_id=at(0, j), device_id_type=MESH,
        )
        for j in range(1, nx)
    ]

    @pl.when(ctx == 0)
    def _():
        for copy in root_copies:
            copy.start()
        anchor_local.start()

    def anchor_arrived(j):
        pltpu.make_async_copy(anc.at[j], anc.at[j], a_recv.at[j]).wait()

    loads[4].wait()
    loads[5].wait()
    my_head = x * hpx + z // pieces_per_head
    lanes = pl.ds(pl.multiple_of(my_head * HEAD_SIZE, HEAD_SIZE), HEAD_SIZE)
    s = dot_nt(pk[...], qq[:, lanes]) * SCALE2
    n_p = pk.shape[0]
    visible = lax.broadcasted_iota(jnp.int32, (n_p, n_q), 0) <= lax.broadcasted_iota(
        jnp.int32, (n_p, n_q), 1
    )
    s = jnp.where(visible, s, NEG_INF)
    self_top = s.max(axis=0, keepdims=True)
    p = jnp.exp2(s - self_top)
    self_s[0:1] = self_top
    self_s[1:2] = p.sum(axis=0, keepdims=True)
    self_o[...] = dot_nn(pv[...].T, p.astype(BF16))

    lax.fori_loop(2, 3, own_head, 0)

    anchor_columns = [
        pltpu.make_async_remote_copy(
            src_ref=anc.at[x], dst_ref=anc.at[x], send_sem=az_send.at[d], recv_sem=a_recv.at[x],
            device_id=at(z_peer(d), x), device_id_type=MESH,
        )
        for d in by_distance(nz)
    ]

    for copy in x_copies:
        copy.wait_recv()
    for i in range(hpx):
        tops = [xrt[d, i, 0:1] for d in range(nx)]
        top = functools.reduce(jnp.maximum, tops)
        weights = [jnp.exp2(t - top) for t in tops]
        zst[i, 0:1] = top
        zst[i, 1:2] = sum(w * xrt[d, i, 1:2] for d, w in enumerate(weights))
        for j in range(pieces_per_head):
            at_piece = i * pieces_per_head + j
            zs[at_piece] = sum(w * xr[d, at_piece].astype(F32) for d, w in enumerate(weights)).astype(BF16)

    z_copies = []
    for d in by_distance(nz):
        zi = z_peer(d)
        z_copies.append(
            pltpu.make_async_remote_copy(
                src_ref=zst.at[zi // pieces_per_head], dst_ref=zrt.at[d],
                send_sem=zt_send.at[d], recv_sem=zt_recv,
                device_id=at(zi, x), device_id_type=MESH,
            )
        )
        z_copies.append(
            pltpu.make_async_remote_copy(
                src_ref=zs.at[zi], dst_ref=zr.at[d], send_sem=zd_send.at[d], recv_sem=zd_recv,
                device_id=at(zi, x), device_id_type=MESH,
            )
        )
    for copy in z_copies:
        copy.start()

    @pl.when(z == 0)
    def _():
        anchor_arrived(x)
        for copy in anchor_columns:
            copy.start()

    lax.fori_loop(3, heads, own_head, 0)
    loads[6].wait()
    wt[...] = wb[...].T

    pltpu.make_async_copy(zrt.at[pl.ds(1, nz - 1)], zrt.at[pl.ds(1, nz - 1)], zt_recv).wait()
    pltpu.make_async_copy(zr.at[pl.ds(1, nz - 1)], zr.at[pl.ds(1, nz - 1)], zd_recv).wait()
    my_stats = zst[z // pieces_per_head]
    tops = [my_stats[0:1]] + [zrt[d, 0:1] for d in range(1, nz)] + [self_s[0:1]]
    top = functools.reduce(jnp.maximum, tops)
    weights = [jnp.exp2(t - top) for t in tops]
    totals = [my_stats[1:2]] + [zrt[d, 1:2] for d in range(1, nz)] + [self_s[1:2]]
    total = sum(w * t for w, t in zip(weights, totals))
    self_rows = self_o[pl.ds(pl.multiple_of(lax.rem(z, pieces_per_head) * rows, rows), rows)]
    sums = weights[-1] * self_rows + weights[0] * zs[z].astype(F32)
    for d in range(1, nz):
        sums = sums + weights[d] * zr[d].astype(F32)
    att[x, z] = (sums * (1.0 / total)).astype(BF16)

    gz_copies = {}
    for d in by_distance(nz):
        gz_copies[d] = pltpu.make_async_remote_copy(
            src_ref=att.at[x, z], dst_ref=att.at[x, z], send_sem=gz_send, recv_sem=gz_recv.at[d],
            device_id=at(z_peer(d), x), device_id_type=MESH,
        )
        gz_copies[d].start()

    def forward(zi):
        for e in by_distance(nx):
            pltpu.make_async_remote_copy(
                src_ref=att.at[x, zi], dst_ref=att.at[x, zi], send_sem=gx_send, recv_sem=gx_recv.at[e],
                device_id=at(z, x_peer(e)), device_id_type=MESH,
            ).start()

    forward(z)
    near_first = by_distance(nz)[::-1]
    anchor_rows = [
        pltpu.make_async_remote_copy(
            src_ref=anc.at[x], dst_ref=anc.at[x], send_sem=ax_send.at[e], recv_sem=a_recv.at[x],
            device_id=at(z, x_peer(e)), device_id_type=MESH,
        )
        for e in by_distance(nx)
    ]
    for step, d in enumerate(near_first):
        zi = lax.rem(z + nz - d, nz)
        pltpu.make_async_copy(att.at[x, zi], att.at[x, zi], gz_recv.at[d]).wait()
        forward(zi)
        if step == len(near_first) // 2:

            @pl.when(z > 0)
            def _():
                anchor_arrived(x)

            for copy in anchor_rows:
                copy.start()

    for e in range(1, nx):
        xi = lax.rem(x + nx - e, nx)
        pltpu.make_async_copy(att.at[xi], att.at[xi], gx_recv.at[e]).wait()

    projected = dot_nn(wt[...], att[...].reshape(heads * HEAD_SIZE, n_q)).T.astype(BF16)
    out_rows = n_q // nh
    for g in range(nh):
        hs[g] = projected[g * out_rows : (g + 1) * out_rows]
    h_copies = []
    for d in range(1, nh):
        gi = lax.rem(head + d, nh)
        copy = pltpu.make_async_remote_copy(
            src_ref=hs.at[gi], dst_ref=hr.at[d], send_sem=h_send.at[d], recv_sem=h_recv,
            device_id={"head": gi}, device_id_type=MESH,
        )
        copy.start()
        h_copies.append(copy)

    for e in range(1, nx):
        anchor_arrived(lax.rem(x + nx - e, nx))
    vat[...] = anc[nx // 2 : nx].reshape(block, HEAD_SIZE).T
    lax.fori_loop(0, heads, anchored_head, 0)

    pltpu.make_async_copy(hr.at[pl.ds(1, nh - 1)], hr.at[pl.ds(1, nh - 1)], h_recv).wait()
    out = hs[head].astype(F32)
    for d in range(1, nh):
        out = out + hr[d].astype(F32)
    out_ref[...] = out.astype(BF16)

    for copy in x_copies + z_copies + h_copies + anchor_rows:
        copy.wait_send()
    pltpu.make_async_copy(zr.at[pl.ds(1, nz - 1)], zr.at[pl.ds(1, nz - 1)], gz_send).wait()
    pltpu.make_async_copy(att.at[pl.ds(1, nx - 1)], att.at[pl.ds(1, nx - 1)], gx_send).wait()

    @pl.when(ctx == 0)
    def _():
        for copy in root_copies:
            copy.wait_send()

    @pl.when(z == 0)
    def _():
        for copy in anchor_columns:
            copy.wait_send()


def solution(mesh):
    nh = mesh.shape["head"]
    n_ctx = mesh.shape["ctx"]
    nx = 4 if n_ctx == 64 else 2
    nz = n_ctx // nx

    def local(dq, k, v, qq, pk, pv, w):
        block, width = dq.shape
        n_q = qq.shape[0]
        heads = width // HEAD_SIZE
        hpx = heads // nx
        rows = hpx * HEAD_SIZE // nz
        out_rows = n_q // nh
        cols = w.shape[1]
        dma = pltpu.SemaphoreType.DMA
        vmem = pltpu.VMEM
        any_spec = pl.BlockSpec(memory_space=pl.ANY)
        vmem_spec = pl.BlockSpec(memory_space=pltpu.VMEM)
        scratch = [
            vmem(dq.shape, BF16), vmem(k.shape, BF16), vmem(v.shape, BF16), vmem(qq.shape, BF16),
            vmem(pk.shape, BF16), vmem(pv.shape, BF16), vmem(w.shape, BF16),
            vmem((cols, width), BF16), vmem((HEAD_SIZE, block), BF16),
            vmem((nx, nz, rows, n_q), BF16), vmem((nx, nz, rows, n_q), BF16),
            vmem((nx, hpx, 2, n_q), F32), vmem((nx, hpx, 2, n_q), F32),
            vmem((nz, rows, n_q), BF16), vmem((nz, rows, n_q), BF16),
            vmem((hpx, 2, n_q), F32), vmem((nz, 2, n_q), F32),
            vmem((nx, nz, rows, n_q), BF16),
            vmem((nh, out_rows, cols), BF16), vmem((nh, out_rows, cols), BF16),
            vmem((HEAD_SIZE, n_q), F32), vmem((2, n_q), F32),
            vmem((heads, HEAD_SIZE, block), F32), vmem((heads, 2, block), F32),
            vmem((nx, 2 * block // nx, HEAD_SIZE), BF16), vmem((HEAD_SIZE, block), BF16),
            dma((7,)), dma((nx,)), dma((nx,)), dma((nx,)), dma((nx,)),
            dma((nz,)), dma(()), dma((nz,)), dma(()),
            dma(()), dma((nz,)), dma(()), dma((nx,)), dma((nh,)), dma(()),
            dma((nx,)), dma((nz,)), dma((nx,)), dma((nx,)),
        ]
        return pl.pallas_call(
            functools.partial(kernel, nx, nz, nh),
            out_shape=(
                jax.ShapeDtypeStruct(dq.shape, BF16),
                jax.ShapeDtypeStruct((out_rows, cols), BF16),
            ),
            in_specs=[any_spec] * 7,
            out_specs=(vmem_spec, vmem_spec),
            scratch_shapes=scratch,
            compiler_params=pltpu.CompilerParams(collective_id=0, has_side_effects=True),
        )(dq, k, v, qq, pk, pv, w)

    placed = (
        P("ctx", "head"),
        P("ctx", "head"),
        P("ctx", "head"),
        P(None, "head"),
        P(None, "head"),
        P(None, "head"),
        P("head", "ctx"),
    )
    return jax.shard_map(
        local,
        mesh=mesh,
        in_specs=placed,
        out_specs=(P("ctx", "head"), P("head", "ctx")),
        check_vma=False,
    )
```

time: 741 us -> 49.7 us (0.07)
  waiting for transfers between devices: 440 us -> 0 us
  blocking collectives: 234 us -> 0 us
  Pallas kernels: 0 us -> 46.4 us
  matrix products: 40.8 us -> 0 us
  between operations: 13.9 us -> 0.65 us
    psum x2 -> x0, waiting for transfers between devices: 418 us -> none  [the longest x1 261 us: from_root(): return lax.psum(block, axis)]
    pmax x1 -> x0, blocking collectives: 123 us -> none  [local(): row_top = lax.pmax(block_max, 'ctx')]
    psum x1 -> x0, blocking collectives: 111 us -> none  [local(): lax.psum((block_total * weights, rescale(block_sums, weights)), 'ctx')]
    pallas_call x0 -> x1, Pallas kernels: none -> 46.4 us  [local(): pl.pallas_call(functools.partial(kernel, nx, nz, nh), out_shape=(jax.Shap...]
    dot_general x65 -> x0, matrix products: 40.8 us -> none  [the longest x32 32.6 us: pair_scores(): lax.dot_general(query_rows, key_rows, (((1,), (1,)), ((), ())), preferred...]
    reduce_scatter x1 -> x0, waiting for transfers between devices: 22 us -> none  [local(): lax.psum_scatter(jnp.dot(attention, out_weight, preferred_element_type=jn...]
  transfers between devices with their start and end apart: 3 -> 0, of which waited for: 3 -> 0; matrix products, arithmetic and copies ran while one was open for 5% -> 0% of each run, Pallas kernels for 0% -> 0%
where the time goes in v1:
time: 49.7 us; the launch traced here: 49.5 us
  Pallas kernels  46.4 us (93%)
  local copies, waits for them, and re-layouts  2.47 us (5%)
  between operations  0.65 us (1%)
    pallas_call x1, Pallas kernels, local(): pl.pallas_call(functools.partial(kernel, nx, nz, nh), out_shape=(jax.Shap...  46.4 us
    unnamed x4, local copies, waits for them, and re-layouts  2.47 us

profile of v1, /device:TPU:1, one launch (start us, length us, event | category | flops | bytes accessed | tf_op | source)
XLA Modules:
  0.0 49.5 jit_solution(14382980551758066879)
XLA Ops:
  0.6 46.4 %shard_map.86 = (bf16[256,1024]{1,0:T(8,128)(2,1)}, bf16[16,128]{1,0:T(8,128)(2,1)}) custom-call(bf16[256,1024]{1,0:T(8,128)(2,1)} %dq_hbm.1, bf16[256,128]{1,0:T(8,128)(2,1)} %k_hbm.1, bf16[256,128]{1,0:T(8,128)(2,1)} %v_hbm.1, bf16[128,1024]{1,0:T(8,128)(2,1)} %qq_hbm.1, bf16[128,128]{1,0:T(8,128)(2,1)} %pk_hbm.1, bf16[128,128]{1,0:T(8,128)(2,1)} %pv_hbm.1, ...), custom_call_target="tpu_custom_call" | custom-call | tf_op jit(solution)/shard_map/pallas_call | solution.py:372
  47.0 0.0 copy-start
  47.1 1.9 %copy.11 = bf16[256,1024]{1,0:T(8,128)(2,1)} copy(bf16[256,1024]{1,0:T(8,128)(2,1)} %get-tuple-element.4) | data formatting | bytes 1048576
  48.9 0.0 copy-done
  48.9 0.6 %copy.12 = bf16[16,128]{1,0:T(8,128)(2,1)} copy(bf16[16,128]{1,0:T(8,128)(2,1)S(1)} %copy-done) | data formatting | bytes 8192
Async XLA Ops:
  47.0 1.9 %copy-start = (bf16[16,128]{1,0:T(8,128)(2,1)S(1)}, bf16[16,128]{1,0:T(8,128)(2,1)}, u32[]{:S(2)}) copy-start(bf16[16,128]{1,0:T(8,128)(2,1)} %get-tuple-element.5) | copy-start | bytes 12292

commit v2 on v1

--- a/solution.py
+++ b/solution.py
@@ -33,12 +33,12 @@
     nx, nz, nh,
     dq_hbm, k_hbm, v_hbm, qq_hbm, pk_hbm, pv_hbm, w_hbm,
     doc_ref, out_ref,
-    dq, kb, vb, qq, pk, pv, wb, wt, vt,
+    dq, kb, vb, qq, pk, pv, wx, vt,
     xs, xr, xst, xrt, zs, zr, zst, zrt, att, hs, hr,
     self_o, self_s, own_o, own_s, anc, vat,
     in_sem, xd_send, xd_recv, xt_send, xt_recv,
     zd_send, zd_recv, zt_send, zt_recv,
-    gz_send, gz_recv, gx_send, gx_recv, h_send, h_recv,
+    gz_send, gz_recv, w_send, w_recv, h_send, h_recv,
     ar_send, az_send, ax_send, a_recv,
 ):
     ctx = lax.axis_index("ctx")
@@ -61,10 +61,18 @@
     def at(zi, xi):
         return {"ctx": zi * nx + xi}
 
+    w_rows = wx.shape[1]
+
+    def w_block(xi):
+        return w_hbm.at[pl.ds(pl.multiple_of(xi * w_rows, w_rows), w_rows)]
+
     loads = [
         pltpu.make_async_copy(src, dst, in_sem.at[i])
         for i, (src, dst) in enumerate(
-            ((k_hbm, kb), (qq_hbm, qq), (v_hbm, vb), (dq_hbm, dq), (pk_hbm, pk), (pv_hbm, pv), (w_hbm, wb))
+            (
+                (k_hbm, kb), (qq_hbm, qq), (v_hbm, vb), (dq_hbm, dq),
+                (pk_hbm, pk), (pv_hbm, pv), (w_block(x), wx.at[0]),
+            )
         )
     ]
     for load in loads:
@@ -73,12 +81,13 @@
     barrier = pltpu.get_barrier_semaphore()
     for d in by_distance(nz):
         pl.semaphore_signal(barrier, inc=1, device_id=at(z_peer(d), x), device_id_type=MESH)
-    for d in by_distance(nx):
-        pl.semaphore_signal(barrier, inc=1, device_id=at(z, x_peer(d)), device_id_type=MESH)
-    for d in range(1, nh):
-        pl.semaphore_signal(
-            barrier, inc=1, device_id={"head": lax.rem(head + d, nh)}, device_id_type=MESH
-        )
+    for d in range(nx):
+        for g in range(nh):
+            if d or g:
+                pl.semaphore_signal(
+                    barrier, inc=1, device_id={**at(z, x_peer(d)), "head": lax.rem(head + g, nh)},
+                    device_id_type=MESH,
+                )
 
     loads[0].wait()
     loads[1].wait()
@@ -99,8 +108,18 @@
             stats[d, i, 0:1] = top
             stats[d, i, 1:2] = total
 
-    for d in by_distance(nx):
+    x_copies = []
+    for step, d in enumerate(by_distance(nx)):
         question_group(d, xs, xst)
+        if step == 0:
+            pl.semaphore_wait(barrier, nx * nh - 1 + nz - 1)
+        for src, dst, send, recv in ((xst, xrt, xt_send, xt_recv), (xs, xr, xd_send, xd_recv)):
+            copy = pltpu.make_async_remote_copy(
+                src_ref=src.at[d], dst_ref=dst.at[d], send_sem=send.at[d], recv_sem=recv.at[d],
+                device_id=at(z, x_peer(d)), device_id_type=MESH,
+            )
+            copy.start()
+            x_copies.append(copy)
     question_group(0, xr, xrt)
 
     key_at = lax.broadcasted_iota(jnp.int32, (block, block), 0)
@@ -130,22 +149,6 @@
         doc_ref[:, lanes] = (o * (1.0 / total)).T.astype(BF16)
         return carry
 
-    loads[3].wait()
-    lax.fori_loop(0, 2, own_head, 0)
-
-    pl.semaphore_wait(barrier, (nx - 1) + (nz - 1) + (nh - 1))
-
-    x_copies = []
-    for d in by_distance(nx):
-        peer = at(z, x_peer(d))
-        for src, dst, send, recv in ((xst, xrt, xt_send, xt_recv), (xs, xr, xd_send, xd_recv)):
-            copy = pltpu.make_async_remote_copy(
-                src_ref=src.at[d], dst_ref=dst.at[d], send_sem=send.at[d], recv_sem=recv.at[d],
-                device_id=peer, device_id_type=MESH,
-            )
-            copy.start()
-            x_copies.append(copy)
-
     a_rows = anc.shape[1]
 
     def anchor_source(j):
@@ -169,6 +172,16 @@
 
     def anchor_arrived(j):
         pltpu.make_async_copy(anc.at[j], anc.at[j], a_recv.at[j]).wait()
+
+    w_copies = [
+        pltpu.make_async_remote_copy(
+            src_ref=w_block(x_peer(d)), dst_ref=wx.at[d], send_sem=w_send.at[d], recv_sem=w_recv.at[d],
+            device_id=at(z, x_peer(d)), device_id_type=MESH,
+        )
+        for d in by_distance(nx)
+    ]
+    for copy in w_copies:
+        copy.start()
 
     loads[4].wait()
     loads[5].wait()
@@ -186,7 +199,8 @@
     self_s[1:2] = p.sum(axis=0, keepdims=True)
     self_o[...] = dot_nn(pv[...].T, p.astype(BF16))
 
-    lax.fori_loop(2, 3, own_head, 0)
+    loads[3].wait()
+    lax.fori_loop(0, 3, own_head, 0)
 
     anchor_columns = [
         pltpu.make_async_remote_copy(
@@ -234,8 +248,6 @@
             copy.start()
 
     lax.fori_loop(3, heads, own_head, 0)
-    loads[6].wait()
-    wt[...] = wb[...].T
 
     pltpu.make_async_copy(zrt.at[pl.ds(1, nz - 1)], zrt.at[pl.ds(1, nz - 1)], zt_recv).wait()
     pltpu.make_async_copy(zr.at[pl.ds(1, nz - 1)], zr.at[pl.ds(1, nz - 1)], zd_recv).wait()
@@ -249,25 +261,18 @@
     sums = weights[-1] * self_rows + weights[0] * zs[z].astype(F32)
     for d in range(1, nz):
         sums = sums + weights[d] * zr[d].astype(F32)
-    att[x, z] = (sums * (1.0 / total)).astype(BF16)
-
-    gz_copies = {}
-    for d in by_distance(nz):
-        gz_copies[d] = pltpu.make_async_remote_copy(
-            src_ref=att.at[x, z], dst_ref=att.at[x, z], send_sem=gz_send, recv_sem=gz_recv.at[d],
+    att[z] = (sums * (1.0 / total)).astype(BF16)
+
+    gz_copies = [
+        pltpu.make_async_remote_copy(
+            src_ref=att.at[z], dst_ref=att.at[z], send_sem=gz_send.at[d], recv_sem=gz_recv,
             device_id=at(z_peer(d), x), device_id_type=MESH,
         )
-        gz_copies[d].start()
-
-    def forward(zi):
-        for e in by_distance(nx):
-            pltpu.make_async_remote_copy(
-                src_ref=att.at[x, zi], dst_ref=att.at[x, zi], send_sem=gx_send, recv_sem=gx_recv.at[e],
-                device_id=at(z, x_peer(e)), device_id_type=MESH,
-            ).start()
-
-    forward(z)
-    near_first = by_distance(nz)[::-1]
+        for d in by_distance(nz)
+    ]
+    for copy in gz_copies:
+        copy.start()
+
     anchor_rows = [
         pltpu.make_async_remote_copy(
             src_ref=anc.at[x], dst_ref=anc.at[x], send_sem=ax_send.at[e], recv_sem=a_recv.at[x],
@@ -275,52 +280,58 @@
         )
         for e in by_distance(nx)
     ]
-    for step, d in enumerate(near_first):
-        zi = lax.rem(z + nz - d, nz)
-        pltpu.make_async_copy(att.at[x, zi], att.at[x, zi], gz_recv.at[d]).wait()
-        forward(zi)
-        if step == len(near_first) // 2:
-
-            @pl.when(z > 0)
-            def _():
-                anchor_arrived(x)
-
-            for copy in anchor_rows:
-                copy.start()
-
-    for e in range(1, nx):
-        xi = lax.rem(x + nx - e, nx)
-        pltpu.make_async_copy(att.at[xi], att.at[xi], gx_recv.at[e]).wait()
-
-    projected = dot_nn(wt[...], att[...].reshape(heads * HEAD_SIZE, n_q)).T.astype(BF16)
+
+    @pl.when(z > 0)
+    def _():
+        anchor_arrived(x)
+
+    for copy in anchor_rows:
+        copy.start()
+    loads[6].wait()
+    for copy in w_copies:
+        copy.wait_recv()
+
+    pltpu.make_async_copy(att.at[pl.ds(0, nz - 1)], att.at[pl.ds(0, nz - 1)], gz_recv).wait()
+
+    attention = att[...].reshape(hpx * HEAD_SIZE, n_q).T
     out_rows = n_q // nh
-    for g in range(nh):
-        hs[g] = projected[g * out_rows : (g + 1) * out_rows]
+    for d in range(0, nx, 2):
+        weights = jnp.concatenate([wx[d], wx[d + 1]], axis=1)
+        projected = dot_nn(attention, weights).astype(BF16)
+        for i in range(2):
+            columns = projected[:, i * wx.shape[2] : (i + 1) * wx.shape[2]]
+            for g in range(nh):
+                hs[d + i, g] = columns[g * out_rows : (g + 1) * out_rows]
     h_copies = []
-    for d in range(1, nh):
-        gi = lax.rem(head + d, nh)
-        copy = pltpu.make_async_remote_copy(
-            src_ref=hs.at[gi], dst_ref=hr.at[d], send_sem=h_send.at[d], recv_sem=h_recv,
-            device_id={"head": gi}, device_id_type=MESH,
-        )
-        copy.start()
-        h_copies.append(copy)
+    for d in by_distance(nx) + [0]:
+        for g in range(nh):
+            if d or g:
+                gi = lax.rem(head + g, nh)
+                h_copies.append(
+                    pltpu.make_async_remote_copy(
+                        src_ref=hs.at[d, gi], dst_ref=hr.at[d * nh + g],
+                        send_sem=h_send, recv_sem=h_recv,
+                        device_id={**at(z, lax.rem(x + nx - d, nx)), "head": gi}, device_id_type=MESH,
+                    )
+                )
+    for copy in h_copies:
+        copy.start()
 
     for e in range(1, nx):
         anchor_arrived(lax.rem(x + nx - e, nx))
     vat[...] = anc[nx // 2 : nx].reshape(block, HEAD_SIZE).T
     lax.fori_loop(0, heads, anchored_head, 0)
 
-    pltpu.make_async_copy(hr.at[pl.ds(1, nh - 1)], hr.at[pl.ds(1, nh - 1)], h_recv).wait()
-    out = hs[head].astype(F32)
-    for d in range(1, nh):
+    others = hr.at[pl.ds(1, nx * nh - 1)]
+    pltpu.make_async_copy(others, others, h_recv).wait()
+    out = hs[0, head].astype(F32)
+    for d in range(1, nx * nh):
         out = out + hr[d].astype(F32)
     out_ref[...] = out.astype(BF16)
 
-    for copy in x_copies + z_copies + h_copies + anchor_rows:
+    for copy in x_copies + w_copies + z_copies + gz_copies + anchor_rows:
         copy.wait_send()
-    pltpu.make_async_copy(zr.at[pl.ds(1, nz - 1)], zr.at[pl.ds(1, nz - 1)], gz_send).wait()
-    pltpu.make_async_copy(att.at[pl.ds(1, nx - 1)], att.at[pl.ds(1, nx - 1)], gx_send).wait()
+    pltpu.make_async_copy(others, others, h_send).wait()
 
     @pl.when(ctx == 0)
     def _():
@@ -331,6 +342,17 @@
     def _():
         for copy in anchor_columns:
             copy.wait_send()
+
+
+def put_out(doc_vmem, out_vmem, doc_hbm, out_hbm, sem):
+    copies = [
+        pltpu.make_async_copy(doc_vmem, doc_hbm, sem.at[0]),
+        pltpu.make_async_copy(out_vmem, out_hbm, sem.at[1]),
+    ]
+    for copy in copies:
+        copy.start()
+    for copy in copies:
+        copy.wait()
 
 
 def solution(mesh):
@@ -353,33 +375,40 @@
         vmem_spec = pl.BlockSpec(memory_space=pltpu.VMEM)
         scratch = [
             vmem(dq.shape, BF16), vmem(k.shape, BF16), vmem(v.shape, BF16), vmem(qq.shape, BF16),
-            vmem(pk.shape, BF16), vmem(pv.shape, BF16), vmem(w.shape, BF16),
-            vmem((cols, width), BF16), vmem((HEAD_SIZE, block), BF16),
+            vmem(pk.shape, BF16), vmem(pv.shape, BF16), vmem((nx, hpx * HEAD_SIZE, cols), BF16),
+            vmem((HEAD_SIZE, block), BF16),
             vmem((nx, nz, rows, n_q), BF16), vmem((nx, nz, rows, n_q), BF16),
             vmem((nx, hpx, 2, n_q), F32), vmem((nx, hpx, 2, n_q), F32),
             vmem((nz, rows, n_q), BF16), vmem((nz, rows, n_q), BF16),
             vmem((hpx, 2, n_q), F32), vmem((nz, 2, n_q), F32),
-            vmem((nx, nz, rows, n_q), BF16),
-            vmem((nh, out_rows, cols), BF16), vmem((nh, out_rows, cols), BF16),
+            vmem((nz, rows, n_q), BF16),
+            vmem((nx, nh, out_rows, cols), BF16), vmem((nx * nh, out_rows, cols), BF16),
             vmem((HEAD_SIZE, n_q), F32), vmem((2, n_q), F32),
             vmem((heads, HEAD_SIZE, block), F32), vmem((heads, 2, block), F32),
             vmem((nx, 2 * block // nx, HEAD_SIZE), BF16), vmem((HEAD_SIZE, block), BF16),
             dma((7,)), dma((nx,)), dma((nx,)), dma((nx,)), dma((nx,)),
             dma((nz,)), dma(()), dma((nz,)), dma(()),
-            dma(()), dma((nz,)), dma(()), dma((nx,)), dma((nh,)), dma(()),
+            dma((nz,)), dma(()), dma((nx,)), dma((nx,)), dma(()), dma(()),
             dma((nx,)), dma((nz,)), dma((nx,)), dma((nx,)),
         ]
-        return pl.pallas_call(
+        results = pl.pallas_call(
             functools.partial(kernel, nx, nz, nh),
-            out_shape=(
-                jax.ShapeDtypeStruct(dq.shape, BF16),
-                jax.ShapeDtypeStruct((out_rows, cols), BF16),
-            ),
-            in_specs=[any_spec] * 7,
+            out_shape=(pltpu.VMEM(dq.shape, BF16), pltpu.VMEM((out_rows, cols), BF16)),
+            in_specs=[pl.BlockSpec(memory_space=pltpu.HBM)] * 7,
             out_specs=(vmem_spec, vmem_spec),
             scratch_shapes=scratch,
-            compiler_params=pltpu.CompilerParams(collective_id=0, has_side_effects=True),
+            compiler_params=pltpu.CompilerParams(
+                collective_id=0, has_side_effects=True, vmem_limit_bytes=67043328 - (560 << 10)
+            ),
         )(dq, k, v, qq, pk, pv, w)
+        return pl.pallas_call(
+            put_out,
+            out_shape=tuple(jax.ShapeDtypeStruct(r.shape, r.dtype) for r in results),
+            in_specs=[vmem_spec] * 2,
+            out_specs=(any_spec, any_spec),
+            scratch_shapes=[dma((2,))],
+            compiler_params=pltpu.CompilerParams(vmem_limit_bytes=4 << 20),
+        )(*results)
 
     placed = (
         P("ctx", "head"),

time: 49.7 us -> 46.6 us (0.938)
  local copies, waits for them, and re-layouts: 2.47 us -> 0 us
  Pallas kernels: 46.4 us -> 45.8 us
    unnamed x4 -> x0, local copies, waits for them, and re-layouts: 2.47 us -> none
    pallas_call x1 -> x2, Pallas kernels: 46.4 us -> 45.8 us  [the longest x1 45 us: local(): pl.pallas_call(functools.partial(kernel, nx, nz, nh), out_shape=(pltpu.VM...]
where the time goes in v2:
time: 46.6 us; the launch traced here: 46.4 us
  Pallas kernels  45.8 us (98%)
  between operations  0.64 us (1%)
    pallas_call x1, Pallas kernels, local(): pl.pallas_call(functools.partial(kernel, nx, nz, nh), out_shape=(pltpu.VM...  45 us

profile of v2, /device:TPU:1, one launch (start us, length us, event | category | flops | bytes accessed | tf_op | source)
XLA Modules:
  0.0 46.4 jit_solution(10024953925096132529)
XLA Ops:
  0.6 45.0 %shard_map.86 = (bf16[256,1024]{1,0:T(8,128)(2,1)S(1)}, bf16[16,128]{1,0:T(8,128)(2,1)S(1)}) custom-call(bf16[256,1024]{1,0:T(8,128)(2,1)} %dq_hbm.1, bf16[256,128]{1,0:T(8,128)(2,1)} %k_hbm.1, bf16[256,128]{1,0:T(8,128)(2,1)} %v_hbm.1, bf16[128,1024]{1,0:T(8,128)(2,1)} %qq_hbm.1, bf16[128,128]{1,0:T(8,128)(2,1)} %pk_hbm.1, bf16[128,128]{1,0:T(8,128)(2,1)} %pv_hbm.1, ...), custom_call_target="tpu_custom_call" | custom-call | tf_op jit(solution)/shard_map/pallas_call | solution.py:394
  45.6 0.8 %shard_map.87 = (bf16[256,1024]{1,0:T(8,128)(2,1)}, bf16[16,128]{1,0:T(8,128)(2,1)}) custom-call(bf16[256,1024]{1,0:T(8,128)(2,1)S(1)} %get-tuple-element.4.doc_vmem, bf16[16,128]{1,0:T(8,128)(2,1)S(1)} %get-tuple-element.5.out_vmem), custom_call_target="tpu_custom_call" | custom-call | tf_op jit(solution)/shard_map/pallas_call | solution.py:404

commit v3 on v2

--- a/solution.py
+++ b/solution.py
@@ -39,7 +39,7 @@
     in_sem, xd_send, xd_recv, xt_send, xt_recv,
     zd_send, zd_recv, zt_send, zt_recv,
     gz_send, gz_recv, w_send, w_recv, h_send, h_recv,
-    ar_send, az_send, ax_send, a_recv,
+    ar_send, az_send, ax_send, a_recv, ready,
 ):
     ctx = lax.axis_index("ctx")
     head = lax.axis_index("head")
@@ -78,9 +78,15 @@
     for load in loads:
         load.start()
 
+    n_early = nz // 4
+    early = z < n_early
     barrier = pltpu.get_barrier_semaphore()
     for d in by_distance(nz):
-        pl.semaphore_signal(barrier, inc=1, device_id=at(z_peer(d), x), device_id_type=MESH)
+
+        @pl.when(early | (z_peer(d) >= n_early))
+        def _():
+            pl.semaphore_signal(barrier, inc=1, device_id=at(z_peer(d), x), device_id_type=MESH)
+
     for d in range(nx):
         for g in range(nh):
             if d or g:
@@ -112,7 +118,17 @@
     for step, d in enumerate(by_distance(nx)):
         question_group(d, xs, xst)
         if step == 0:
-            pl.semaphore_wait(barrier, nx * nh - 1 + nz - 1)
+
+            @pl.when(early)
+            def _():
+                pl.semaphore_wait(barrier, nx * nh - 1 + n_early - 1)
+
+            @pl.when(jnp.logical_not(early))
+            def _():
+                pl.semaphore_wait(barrier, nx * nh - 1 + nz - 1)
+                for zi in range(n_early):
+                    pl.semaphore_signal(ready, inc=1, device_id=at(zi, x), device_id_type=MESH)
+
         for src, dst, send, recv in ((xst, xrt, xt_send, xt_recv), (xs, xr, xd_send, xd_recv)):
             copy = pltpu.make_async_remote_copy(
                 src_ref=src.at[d], dst_ref=dst.at[d], send_sem=send.at[d], recv_sem=recv.at[d],
@@ -180,9 +196,6 @@
         )
         for d in by_distance(nx)
     ]
-    for copy in w_copies:
-        copy.start()
-
     loads[4].wait()
     loads[5].wait()
     my_head = x * hpx + z // pieces_per_head
@@ -200,15 +213,61 @@
     self_o[...] = dot_nn(pv[...].T, p.astype(BF16))
 
     loads[3].wait()
-    lax.fori_loop(0, 3, own_head, 0)
-
-    anchor_columns = [
+
+    def own_heads(first, last):
+        lax.fori_loop(first, last, own_head, 0)
+
+    own_heads(0, 3)
+
+    def anchor_column(zi):
+        return pltpu.make_async_remote_copy(
+            src_ref=anc.at[x], dst_ref=anc.at[x], send_sem=az_send.at[zi], recv_sem=a_recv.at[x],
+            device_id=at(zi, x), device_id_type=MESH,
+        )
+
+    passes = {0: list(range(1, nz))}
+    if nz == 16:
+        passes = {0: [1, 2, 3, 12, 15], 3: [8, 4], 4: [6, 5], 8: [9, 7], 12: [10, 11], 15: [13, 14]}
+    anchor_columns = {
+        zi: ([anchor_column(t) for t in to if t < n_early], [anchor_column(t) for t in to if t >= n_early])
+        for zi, to in passes.items()
+    }
+
+    def send_anchor(sources):
+        for zi in sources:
+            if zi in anchor_columns:
+
+                @pl.when(z == zi)
+                def _():
+                    for copy in anchor_columns[zi][1]:
+                        copy.start()
+
+    anchor_rows = [
         pltpu.make_async_remote_copy(
-            src_ref=anc.at[x], dst_ref=anc.at[x], send_sem=az_send.at[d], recv_sem=a_recv.at[x],
-            device_id=at(z_peer(d), x), device_id_type=MESH,
-        )
-        for d in by_distance(nz)
-    ]
+            src_ref=anc.at[x], dst_ref=anc.at[x], send_sem=ax_send.at[e], recv_sem=a_recv.at[x],
+            device_id=at(z, x_peer(e)), device_id_type=MESH,
+        )
+        for e in by_distance(nx)
+    ]
+    other_blocks = [lax.rem(x + nx - e, nx) for e in range(1, nx)]
+
+    def spread_anchor():
+        anchor_arrived(x)
+
+        @pl.when(z == 0)
+        def _():
+            for copy in anchor_columns[0][0]:
+                copy.start()
+
+        send_anchor(range(n_early, nz))
+        for copy in anchor_rows:
+            copy.start()
+
+    def anchored_heads():
+        for j in other_blocks:
+            anchor_arrived(j)
+        vat[...] = anc[nx // 2 : nx].reshape(block, HEAD_SIZE).T
+        lax.fori_loop(0, heads, anchored_head, 0)
 
     for copy in x_copies:
         copy.wait_recv()
@@ -238,16 +297,27 @@
                 device_id=at(zi, x), device_id_type=MESH,
             )
         )
+
+    @pl.when(early)
+    def _():
+        spread_anchor()
+        own_heads(3, heads)
+        pl.semaphore_wait(ready, nz - n_early)
+
     for copy in z_copies:
         copy.start()
 
-    @pl.when(z == 0)
-    def _():
-        anchor_arrived(x)
-        for copy in anchor_columns:
-            copy.start()
-
-    lax.fori_loop(3, heads, own_head, 0)
+    send_anchor(range(n_early))
+    for copy in w_copies:
+        copy.start()
+
+    @pl.when(early)
+    def _():
+        anchored_heads()
+
+    @pl.when(jnp.logical_not(early))
+    def _():
+        own_heads(3, heads)
 
     pltpu.make_async_copy(zrt.at[pl.ds(1, nz - 1)], zrt.at[pl.ds(1, nz - 1)], zt_recv).wait()
     pltpu.make_async_copy(zr.at[pl.ds(1, nz - 1)], zr.at[pl.ds(1, nz - 1)], zd_recv).wait()
@@ -273,20 +343,10 @@
     for copy in gz_copies:
         copy.start()
 
-    anchor_rows = [
-        pltpu.make_async_remote_copy(
-            src_ref=anc.at[x], dst_ref=anc.at[x], send_sem=ax_send.at[e], recv_sem=a_recv.at[x],
-            device_id=at(z, x_peer(e)), device_id_type=MESH,
-        )
-        for e in by_distance(nx)
-    ]
-
-    @pl.when(z > 0)
-    def _():
-        anchor_arrived(x)
-
-    for copy in anchor_rows:
-        copy.start()
+    @pl.when(jnp.logical_not(early))
+    def _():
+        spread_anchor()
+
     loads[6].wait()
     for copy in w_copies:
         copy.wait_recv()
@@ -295,32 +355,28 @@
 
     attention = att[...].reshape(hpx * HEAD_SIZE, n_q).T
     out_rows = n_q // nh
-    for d in range(0, nx, 2):
-        weights = jnp.concatenate([wx[d], wx[d + 1]], axis=1)
+    far_first = by_distance(nx) + [0]
+    for pair in (far_first[:2], far_first[2:]) if nx > 2 else (far_first,):
+        weights = jnp.concatenate([wx[d] for d in pair], axis=1)
         projected = dot_nn(attention, weights).astype(BF16)
-        for i in range(2):
+        for i, d in enumerate(pair):
             columns = projected[:, i * wx.shape[2] : (i + 1) * wx.shape[2]]
             for g in range(nh):
-                hs[d + i, g] = columns[g * out_rows : (g + 1) * out_rows]
-    h_copies = []
-    for d in by_distance(nx) + [0]:
-        for g in range(nh):
-            if d or g:
-                gi = lax.rem(head + g, nh)
-                h_copies.append(
-                    pltpu.make_async_remote_copy(
+                hs[d, g] = columns[g * out_rows : (g + 1) * out_rows]
+            for g in sorted(range(nh), key=lambda g: -min(g, nh - g)):
+                if d or g:
+                    gi = lax.rem(head + g, nh)
+                    copy = pltpu.make_async_remote_copy(
                         src_ref=hs.at[d, gi], dst_ref=hr.at[d * nh + g],
                         send_sem=h_send, recv_sem=h_recv,
-                        device_id={**at(z, lax.rem(x + nx - d, nx)), "head": gi}, device_id_type=MESH,
+                        device_id={**at(z, lax.rem(x + nx - d, nx)), "head": gi},
+                        device_id_type=MESH,
                     )
-                )
-    for copy in h_copies:
-        copy.start()
-
-    for e in range(1, nx):
-        anchor_arrived(lax.rem(x + nx - e, nx))
-    vat[...] = anc[nx // 2 : nx].reshape(block, HEAD_SIZE).T
-    lax.fori_loop(0, heads, anchored_head, 0)
+                    copy.start()
+
+    @pl.when(jnp.logical_not(early))
+    def _():
+        anchored_heads()
 
     others = hr.at[pl.ds(1, nx * nh - 1)]
     pltpu.make_async_copy(others, others, h_recv).wait()
@@ -338,10 +394,12 @@
         for copy in root_copies:
             copy.wait_send()
 
-    @pl.when(z == 0)
-    def _():
-        for copy in anchor_columns:
-            copy.wait_send()
+    for zi, (near, far) in anchor_columns.items():
+
+        @pl.when(z == zi)
+        def _():
+            for copy in near + far:
+                copy.wait_send()
 
 
 def put_out(doc_vmem, out_vmem, doc_hbm, out_hbm, sem):
@@ -390,6 +448,7 @@
             dma((nz,)), dma(()), dma((nz,)), dma(()),
             dma((nz,)), dma(()), dma((nx,)), dma((nx,)), dma(()), dma(()),
             dma((nx,)), dma((nz,)), dma((nx,)), dma((nx,)),
+            pltpu.SemaphoreType.REGULAR,
         ]
         results = pl.pallas_call(
             functools.partial(kernel, nx, nz, nh),

time: 46.6 us -> 44.2 us (0.948)
  Pallas kernels: 45.8 us -> 43.4 us
    pallas_call x1, Pallas kernels: 45 us -> 42.6 us  [local(): pl.pallas_call(functools.partial(kernel, nx, nz, nh), out_shape=(pltpu.VM...]
where the time goes in v3:
time: 44.2 us; the launch traced here: 44.1 us
  Pallas kernels  43.4 us (98%)
  between operations  0.64 us (1%)
    pallas_call x1, Pallas kernels, local(): pl.pallas_call(functools.partial(kernel, nx, nz, nh), out_shape=(pltpu.VM...  42.6 us

profile of v3, /device:TPU:1, one launch (start us, length us, event | category | flops | bytes accessed | tf_op | source)
XLA Modules:
  0.0 44.1 jit_solution(8289214799856629500)
XLA Ops:
  0.6 42.6 %shard_map.86 = (bf16[256,1024]{1,0:T(8,128)(2,1)S(1)}, bf16[16,128]{1,0:T(8,128)(2,1)S(1)}) custom-call(bf16[256,1024]{1,0:T(8,128)(2,1)} %dq_hbm.1, bf16[256,128]{1,0:T(8,128)(2,1)} %k_hbm.1, bf16[256,128]{1,0:T(8,128)(2,1)} %v_hbm.1, bf16[128,1024]{1,0:T(8,128)(2,1)} %qq_hbm.1, bf16[128,128]{1,0:T(8,128)(2,1)} %pk_hbm.1, bf16[128,128]{1,0:T(8,128)(2,1)} %pv_hbm.1, ...), custom_call_target="tpu_custom_call" | custom-call | tf_op jit(solution)/shard_map/pallas_call | solution.py:453
  43.3 0.8 %shard_map.87 = (bf16[256,1024]{1,0:T(8,128)(2,1)}, bf16[16,128]{1,0:T(8,128)(2,1)}) custom-call(bf16[256,1024]{1,0:T(8,128)(2,1)S(1)} %get-tuple-element.4.doc_vmem, bf16[16,128]{1,0:T(8,128)(2,1)S(1)} %get-tuple-element.5.out_vmem), custom_call_target="tpu_custom_call" | custom-call | tf_op jit(solution)/shard_map/pallas_call | solution.py:463

commit v4 on v3

--- a/solution.py
+++ b/solution.py
@@ -34,11 +34,11 @@
     dq_hbm, k_hbm, v_hbm, qq_hbm, pk_hbm, pv_hbm, w_hbm,
     doc_ref, out_ref,
     dq, kb, vb, qq, pk, pv, wx, vt,
-    xs, xr, xst, xrt, zs, zr, zst, zrt, att, hs, hr,
+    xs, xr, xst, xrt, zs, zr, zst, zrt, att, hs, hp, h2, hr,
     self_o, self_s, own_o, own_s, anc, vat,
     in_sem, xd_send, xd_recv, xt_send, xt_recv,
     zd_send, zd_recv, zt_send, zt_recv,
-    gz_send, gz_recv, w_send, w_recv, h_send, h_recv,
+    gz_send, gz_recv, w_send, w_recv, p_send, p_recv, h_send, h_recv,
     ar_send, az_send, ax_send, a_recv, ready,
 ):
     ctx = lax.axis_index("ctx")
@@ -78,7 +78,7 @@
     for load in loads:
         load.start()
 
-    n_early = nz // 4
+    n_early = max(1, nz // 4)
     early = z < n_early
     barrier = pltpu.get_barrier_semaphore()
     for d in by_distance(nz):
@@ -87,13 +87,18 @@
         def _():
             pl.semaphore_signal(barrier, inc=1, device_id=at(z_peer(d), x), device_id_type=MESH)
 
+    ny = nh // 2
+    core = lax.rem(head, 2)
+    partner = {"head": head + 1 - 2 * core}
+
+    def plane_peer(d, gy):
+        return {**at(z, lax.rem(x + nx - d, nx)), "head": lax.rem(head // 2 + gy, ny) * 2 + core}
+
+    pl.semaphore_signal(barrier, inc=1, device_id=partner, device_id_type=MESH)
     for d in range(nx):
-        for g in range(nh):
-            if d or g:
-                pl.semaphore_signal(
-                    barrier, inc=1, device_id={**at(z, x_peer(d)), "head": lax.rem(head + g, nh)},
-                    device_id_type=MESH,
-                )
+        for gy in range(ny):
+            if d or gy:
+                pl.semaphore_signal(barrier, inc=1, device_id=plane_peer(d, gy), device_id_type=MESH)
 
     loads[0].wait()
     loads[1].wait()
@@ -121,11 +126,11 @@
 
             @pl.when(early)
             def _():
-                pl.semaphore_wait(barrier, nx * nh - 1 + n_early - 1)
+                pl.semaphore_wait(barrier, nx * ny + n_early - 1)
 
             @pl.when(jnp.logical_not(early))
             def _():
-                pl.semaphore_wait(barrier, nx * nh - 1 + nz - 1)
+                pl.semaphore_wait(barrier, nx * ny + nz - 1)
                 for zi in range(n_early):
                     pl.semaphore_signal(ready, inc=1, device_id=at(zi, x), device_id_type=MESH)
 
@@ -275,8 +280,10 @@
         tops = [xrt[d, i, 0:1] for d in range(nx)]
         top = functools.reduce(jnp.maximum, tops)
         weights = [jnp.exp2(t - top) for t in tops]
-        zst[i, 0:1] = top
-        zst[i, 1:2] = sum(w * xrt[d, i, 1:2] for d, w in enumerate(weights))
+        total = sum(w * xrt[d, i, 1:2] for d, w in enumerate(weights))
+        zst[i] = top + jnp.log(total) * LOG2E
+        share = 1.0 / total
+        weights = [w * share for w in weights]
         for j in range(pieces_per_head):
             at_piece = i * pieces_per_head + j
             zs[at_piece] = sum(w * xr[d, at_piece].astype(F32) for d, w in enumerate(weights)).astype(BF16)
@@ -322,11 +329,10 @@
     pltpu.make_async_copy(zrt.at[pl.ds(1, nz - 1)], zrt.at[pl.ds(1, nz - 1)], zt_recv).wait()
     pltpu.make_async_copy(zr.at[pl.ds(1, nz - 1)], zr.at[pl.ds(1, nz - 1)], zd_recv).wait()
     my_stats = zst[z // pieces_per_head]
-    tops = [my_stats[0:1]] + [zrt[d, 0:1] for d in range(1, nz)] + [self_s[0:1]]
+    tops = [my_stats] + [zrt[d] for d in range(1, nz)] + [self_s[0:1]]
     top = functools.reduce(jnp.maximum, tops)
     weights = [jnp.exp2(t - top) for t in tops]
-    totals = [my_stats[1:2]] + [zrt[d, 1:2] for d in range(1, nz)] + [self_s[1:2]]
-    total = sum(w * t for w, t in zip(weights, totals))
+    total = sum(weights[:-1]) + weights[-1] * self_s[1:2]
     self_rows = self_o[pl.ds(pl.multiple_of(lax.rem(z, pieces_per_head) * rows, rows), rows)]
     sums = weights[-1] * self_rows + weights[0] * zs[z].astype(F32)
     for d in range(1, nz):
@@ -356,36 +362,47 @@
     attention = att[...].reshape(hpx * HEAD_SIZE, n_q).T
     out_rows = n_q // nh
     far_first = by_distance(nx) + [0]
-    for pair in (far_first[:2], far_first[2:]) if nx > 2 else (far_first,):
+    pairs = [far_first[i : i + 2] for i in range(0, nx, 2)]
+    halves = []
+    for at_pair, pair in enumerate(pairs):
         weights = jnp.concatenate([wx[d] for d in pair], axis=1)
         projected = dot_nn(attention, weights).astype(BF16)
         for i, d in enumerate(pair):
             columns = projected[:, i * wx.shape[2] : (i + 1) * wx.shape[2]]
             for g in range(nh):
-                hs[d, g] = columns[g * out_rows : (g + 1) * out_rows]
-            for g in sorted(range(nh), key=lambda g: -min(g, nh - g)):
-                if d or g:
-                    gi = lax.rem(head + g, nh)
-                    copy = pltpu.make_async_remote_copy(
-                        src_ref=hs.at[d, gi], dst_ref=hr.at[d * nh + g],
+                hs[at_pair, g % 2, i * ny + g // 2] = columns[g * out_rows : (g + 1) * out_rows]
+        half = pltpu.make_async_remote_copy(
+            src_ref=hs.at[at_pair, 1 - core], dst_ref=hp.at[at_pair],
+            send_sem=p_send.at[at_pair], recv_sem=p_recv.at[at_pair],
+            device_id=partner, device_id_type=MESH,
+        )
+        half.start()
+        halves.append(half)
+    for at_pair, pair in enumerate(pairs):
+        halves[at_pair].wait_recv()
+        h2[at_pair] = (hs[at_pair, core].astype(F32) + hp[at_pair].astype(F32)).astype(BF16)
+        for i, d in enumerate(pair):
+            for gy in sorted(range(ny), key=lambda g: -min(g, ny - g)):
+                if d or gy:
+                    pltpu.make_async_remote_copy(
+                        src_ref=h2.at[at_pair, i * ny + lax.rem(head // 2 + gy, ny)],
+                        dst_ref=hr.at[d * ny + gy],
                         send_sem=h_send, recv_sem=h_recv,
-                        device_id={**at(z, lax.rem(x + nx - d, nx)), "head": gi},
-                        device_id_type=MESH,
-                    )
-                    copy.start()
+                        device_id=plane_peer(d, gy), device_id_type=MESH,
+                    ).start()
 
     @pl.when(jnp.logical_not(early))
     def _():
         anchored_heads()
 
-    others = hr.at[pl.ds(1, nx * nh - 1)]
+    others = hr.at[pl.ds(1, nx * ny - 1)]
     pltpu.make_async_copy(others, others, h_recv).wait()
-    out = hs[0, head].astype(F32)
-    for d in range(1, nx * nh):
+    out = h2[len(pairs) - 1, ny + head // 2].astype(F32)
+    for d in range(1, nx * ny):
         out = out + hr[d].astype(F32)
     out_ref[...] = out.astype(BF16)
 
-    for copy in x_copies + w_copies + z_copies + gz_copies + anchor_rows:
+    for copy in x_copies + w_copies + z_copies + gz_copies + anchor_rows + halves:
         copy.wait_send()
     pltpu.make_async_copy(others, others, h_send).wait()
 
@@ -403,10 +420,11 @@
 
 
 def put_out(doc_vmem, out_vmem, doc_hbm, out_hbm, sem):
-    copies = [
-        pltpu.make_async_copy(doc_vmem, doc_hbm, sem.at[0]),
-        pltpu.make_async_copy(out_vmem, out_hbm, sem.at[1]),
-    ]
+    part = doc_vmem.shape[0] // 4
+    copies = [pltpu.make_async_copy(out_vmem, out_hbm, sem.at[4])]
+    for i in range(4):
+        rows = pl.ds(i * part, part)
+        copies.append(pltpu.make_async_copy(doc_vmem.at[rows], doc_hbm.at[rows], sem.at[i]))
     for copy in copies:
         copy.start()
     for copy in copies:
@@ -438,15 +456,16 @@
             vmem((nx, nz, rows, n_q), BF16), vmem((nx, nz, rows, n_q), BF16),
             vmem((nx, hpx, 2, n_q), F32), vmem((nx, hpx, 2, n_q), F32),
             vmem((nz, rows, n_q), BF16), vmem((nz, rows, n_q), BF16),
-            vmem((hpx, 2, n_q), F32), vmem((nz, 2, n_q), F32),
+            vmem((hpx, 1, n_q), F32), vmem((nz, 1, n_q), F32),
             vmem((nz, rows, n_q), BF16),
-            vmem((nx, nh, out_rows, cols), BF16), vmem((nx * nh, out_rows, cols), BF16),
+            vmem((nx // 2, 2, nh, out_rows, cols), BF16), vmem((nx // 2, nh, out_rows, cols), BF16),
+            vmem((nx // 2, nh, out_rows, cols), BF16), vmem((nx * nh // 2, out_rows, cols), BF16),
             vmem((HEAD_SIZE, n_q), F32), vmem((2, n_q), F32),
             vmem((heads, HEAD_SIZE, block), F32), vmem((heads, 2, block), F32),
             vmem((nx, 2 * block // nx, HEAD_SIZE), BF16), vmem((HEAD_SIZE, block), BF16),
             dma((7,)), dma((nx,)), dma((nx,)), dma((nx,)), dma((nx,)),
             dma((nz,)), dma(()), dma((nz,)), dma(()),
-            dma((nz,)), dma(()), dma((nx,)), dma((nx,)), dma(()), dma(()),
+            dma((nz,)), dma(()), dma((nx,)), dma((nx,)), dma((nx // 2,)), dma((nx // 2,)), dma(()), dma(()),
             dma((nx,)), dma((nz,)), dma((nx,)), dma((nx,)),
             pltpu.SemaphoreType.REGULAR,
         ]
@@ -465,7 +484,7 @@
             out_shape=tuple(jax.ShapeDtypeStruct(r.shape, r.dtype) for r in results),
             in_specs=[vmem_spec] * 2,
             out_specs=(any_spec, any_spec),
-            scratch_shapes=[dma((2,))],
+            scratch_shapes=[dma((5,))],
             compiler_params=pltpu.CompilerParams(vmem_limit_bytes=4 << 20),
         )(*results)
 

time: 44.2 us -> 44.1 us (level)
  no operation moved by 1% of the time
where the time goes in v4:
time: 44.1 us; the launch traced here: 44 us
  Pallas kernels  43.4 us (98%)
  between operations  0.64 us (1%)
    pallas_call x1, Pallas kernels, local(): pl.pallas_call(functools.partial(kernel, nx, nz, nh), out_shape=(pltpu.VM...  42.5 us

profile of v4, /device:TPU:1, one launch (start us, length us, event | category | flops | bytes accessed | tf_op | source)
XLA Modules:
  0.0 44.0 jit_solution(18214546922155780861)
XLA Ops:
  0.6 42.5 %shard_map.86 = (bf16[256,1024]{1,0:T(8,128)(2,1)S(1)}, bf16[16,128]{1,0:T(8,128)(2,1)S(1)}) custom-call(bf16[256,1024]{1,0:T(8,128)(2,1)} %dq_hbm.1, bf16[256,128]{1,0:T(8,128)(2,1)} %k_hbm.1, bf16[256,128]{1,0:T(8,128)(2,1)} %v_hbm.1, bf16[128,1024]{1,0:T(8,128)(2,1)} %qq_hbm.1, bf16[128,128]{1,0:T(8,128)(2,1)} %pk_hbm.1, bf16[128,128]{1,0:T(8,128)(2,1)} %pv_hbm.1, ...), custom_call_target="tpu_custom_call" | custom-call | tf_op jit(solution)/shard_map/pallas_call | solution.py:472
  43.2 0.8 %shard_map.87 = (bf16[256,1024]{1,0:T(8,128)(2,1)}, bf16[16,128]{1,0:T(8,128)(2,1)}) custom-call(bf16[256,1024]{1,0:T(8,128)(2,1)S(1)} %get-tuple-element.4.doc_vmem, bf16[16,128]{1,0:T(8,128)(2,1)S(1)} %get-tuple-element.5.out_vmem), custom_call_target="tpu_custom_call" | custom-call | tf_op jit(solution)/shard_map/pallas_call | solution.py:482
